TPU v7x, 1024 devices: a whole 4x8x16 slice. The times are simulated.
1024 devices in a mesh: dp: 16 (over z_hi, x), pipe: 8 (over z_lo, core), seq: 8 (over y).
Axes of the slice: x: 4, y: 8, z: 16 (z_hi: 4, z_lo: 4; z = z_hi * 4 + z_lo), core: 2. Of those that a mesh axis runs over, the one named last changes fastest.
Arguments:
- fwd_input: bfloat16 [8, 16, 1024, 2048], P('pipe', 'dp', 'seq'), may hold values from -6 to 6
- saved_input: bfloat16 [8, 16, 1024, 2048], P('pipe', 'dp', 'seq'), may hold values from -6 to 6
- out_grad: bfloat16 [8, 16, 1024, 2048], P('pipe', 'dp', 'seq'), may hold values from -6 to 6
- fwd_sky: int32 [8, 16, 1024], P('pipe', 'dp'), may hold values 0 or 1
- bwd_sky: int32 [8, 16, 1024], P('pipe', 'dp'), may hold values 0 or 1
- norm_gain: float32 [8, 2048], P('pipe'), may hold values from 0.5 to 1.5
- query_scale: float32 [8, 2048], P('pipe'), may hold values from -4 to 4
- key_scale: float32 [8, 2048], P('pipe'), may hold values from -4 to 4
- value_scale: float32 [8, 2048], P('pipe'), may hold values from -4 to 4
- sky_bias: float32 [8, 16], P('pipe'), may hold values from -4 to 2
Outputs:
- fwd_output: bfloat16 [8, 16, 1024, 2048], P('pipe', 'dp', 'seq')
- bwd_output: bfloat16 [8, 16, 1024, 2048], P('pipe', 'dp', 'seq')
- scale_grads: float32 [8, 4, 2048], P('pipe', None, 'seq')
- bias_grad: float32 [8, 16], P('pipe', 'seq')
All inputs are finite; a program needn't handle non-finite values. No bound on the sum of `fwd_sky` or of `bwd_sky` on one device may be relied on, other than what follows from the above.
Results may differ from a plain program's by a relative error of at most 0.0085.
The roundings to bfloat16 on the way count: a program that leaves them out, or rounds other values in their place, can miss the bound.
Values may be sent and summed in bfloat16 or wider, within the bound.
A program may use at most 32 MiB of HBM per device.

v0:
```python
import math

import jax
import jax.numpy as jnp
from jax import lax
from jax.sharding import PartitionSpec as P

D = 2048
HEAD_DIM = 128


epsilon = 1e-05


def from_behind(shard, axis, by):
    size = lax.axis_size(axis)
    return lax.ppermute(shard, axis, [(i, (i + by) % size) for i in range(size)])


def project(rows, sum_squares, gains):
    norm_g, query_g, key_g, value_g = gains
    rows_f = rows.astype(jnp.float32)
    inv_root = lax.rsqrt(sum_squares[:, None] / D + epsilon)
    scaled = rows_f * inv_root
    normed = scaled * norm_g
    queries = (normed * query_g).astype(jnp.bfloat16)
    keys_low = (normed * key_g).astype(jnp.bfloat16)
    values_low = (normed * value_g).astype(jnp.bfloat16)
    return (scaled, normed, inv_root, queries, keys_low, values_low)


def window_of(rows, block):
    blocks = rows.reshape((8, block) + rows.shape[1:])
    previous = jnp.concatenate([jnp.zeros_like(blocks[:1]), blocks[:-1]], axis=0)
    return jnp.concatenate([previous, blocks], axis=1)


def fold_window(window_grads, block):
    later = window_grads[:, block:]
    earlier = jnp.concatenate(
        [window_grads[1:, :block], jnp.zeros_like(window_grads[:1, :block])], axis=0
    )
    return later + earlier


def window_mask(block):
    inner = jnp.arange(block)[:, None]
    outer = jnp.arange(2 * block)[None, :]
    inside = (outer > inner) & (outer <= inner + block)
    first = jnp.arange(8)[:, None, None] > 0
    return inside[None] & (first | (outer >= block)[None])


def scores_of(query_blocks, key_window, head_bias, sky_window, block):
    factor = 1.0 / math.sqrt(HEAD_DIM)
    scores = (
        jnp.einsum("bthd,buhd->bhtu", query_blocks, key_window, preferred_element_type=jnp.float32)
        * factor
    )
    scores = scores + head_bias[None, :, None, None] * sky_window[:, None, None, :]
    return jnp.where(window_mask(block)[:, None], scores, -1e30)


def attend(query_rows, key_rows, value_rows, head_bias, sky_row):
    length, channels = query_rows.shape
    head_count = channels // HEAD_DIM
    block = length // 8
    query_blocks = query_rows.reshape(8, block, head_count, HEAD_DIM)
    key_window = window_of(key_rows.reshape(length, head_count, HEAD_DIM), block)
    value_window = window_of(value_rows.reshape(length, head_count, HEAD_DIM), block)
    sky_window = window_of(sky_row.astype(jnp.float32), block)
    scores = scores_of(query_blocks, key_window, head_bias, sky_window, block)
    probs_low = jax.nn.softmax(scores, axis=-1).astype(jnp.bfloat16)
    weighted = jnp.einsum(
        "bhtu,buhd->bthd", probs_low, value_window, preferred_element_type=jnp.float32
    )
    return weighted.astype(jnp.bfloat16).reshape(length, channels)


def attend_back(query_rows, key_rows, value_rows, upstream_rows, head_bias, sky_row):
    length, channels = query_rows.shape
    head_count = channels // HEAD_DIM
    block = length // 8
    factor = 1.0 / math.sqrt(HEAD_DIM)
    query_blocks = query_rows.reshape(8, block, head_count, HEAD_DIM)
    upstream_blocks = upstream_rows.reshape(8, block, head_count, HEAD_DIM)
    key_window = window_of(key_rows.reshape(length, head_count, HEAD_DIM), block)
    value_window = window_of(value_rows.reshape(length, head_count, HEAD_DIM), block)
    sky_window = window_of(sky_row.astype(jnp.float32), block)
    scores = scores_of(query_blocks, key_window, head_bias, sky_window, block)
    probs = jax.nn.softmax(scores, axis=-1)
    probs_low = probs.astype(jnp.bfloat16)
    value_part = jnp.einsum(
        "bhtu,bthd->buhd", probs_low, upstream_blocks, preferred_element_type=jnp.float32
    )
    prob_grad = jnp.einsum(
        "bthd,buhd->bhtu", upstream_blocks, value_window, preferred_element_type=jnp.float32
    )
    score_grad = probs * (prob_grad - jnp.sum(probs * prob_grad, axis=-1, keepdims=True))
    bias_part = jnp.sum(score_grad * sky_window[:, None, None, :], axis=(0, 2, 3))
    score_low = score_grad.astype(jnp.bfloat16)
    query_grad = (
        jnp.einsum("bhtu,buhd->bthd", score_low, key_window, preferred_element_type=jnp.float32)
        * factor
    )
    key_part = (
        jnp.einsum("bhtu,bthd->buhd", score_low, query_blocks, preferred_element_type=jnp.float32)
        * factor
    )
    query_low = query_grad.reshape(length, channels).astype(jnp.bfloat16)
    key_low = fold_window(key_part, block).reshape(length, channels).astype(jnp.bfloat16)
    value_low = fold_window(value_part, block).reshape(length, channels).astype(jnp.bfloat16)
    return (query_low, key_low, value_low, bias_part)


def tail_start(query_low, key_low, value_low, scaled, normed, gains):
    norm_g, query_g, key_g, value_g = gains
    query_f = query_low.astype(jnp.float32)
    key_f = key_low.astype(jnp.float32)
    value_f = value_low.astype(jnp.float32)
    normed_grad = query_f * query_g + key_f * key_g + value_f * value_g
    scaled_grad = normed_grad * norm_g
    partials = jnp.stack(
        [
            jnp.sum(normed_grad * scaled, axis=0),
            jnp.sum(query_f * normed, axis=0),
            jnp.sum(key_f * normed, axis=0),
            jnp.sum(value_f * normed, axis=0),
        ]
    )
    local_mix = jnp.sum(scaled_grad * scaled, axis=-1)
    return (scaled_grad, partials, local_mix)


def finish(upstream, scaled_grad, scaled, inv_root, mix_sum):
    result = upstream.astype(jnp.float32) + inv_root * (
        scaled_grad - scaled * (mix_sum[:, None] / D)
    )
    return result.astype(jnp.bfloat16)


def squares(rows):
    rows_f = rows.astype(jnp.float32)
    return jnp.sum(rows_f * rows_f, axis=-1)


def on_device(
    fwd_input,
    saved_input,
    out_grad,
    fwd_sky,
    bwd_sky,
    norm_gain,
    query_scale,
    key_scale,
    value_scale,
    sky_bias,
):
    forward_rows = fwd_input[0, 0]
    stored_rows = saved_input[0, 0]
    upstream = out_grad[0, 0]
    sky_forward = fwd_sky[0, 0]
    sky_backward = bwd_sky[0, 0]
    gains_full = (norm_gain[0], query_scale[0], key_scale[0], value_scale[0])
    shard_width = forward_rows.shape[1] // lax.axis_size("seq")
    local_heads = shard_width // HEAD_DIM
    bias_local = lax.dynamic_slice_in_dim(
        sky_bias[0], lax.axis_index("seq") * local_heads, local_heads
    )
    scaled, normed, inv_root, queries, keys_low, values_low = project(
        forward_rows, squares(forward_rows), gains_full
    )
    query_heads, key_heads, value_heads = (
        lax.all_to_all(queries, "seq", split_axis=1, concat_axis=0, tiled=True),
        lax.all_to_all(keys_low, "seq", split_axis=1, concat_axis=0, tiled=True),
        lax.all_to_all(values_low, "seq", split_axis=1, concat_axis=0, tiled=True),
    )
    attended = attend(query_heads, key_heads, value_heads, bias_local, sky_forward)
    attended_rows = lax.all_to_all(attended, "seq", split_axis=0, concat_axis=1, tiled=True)
    section_result = (forward_rows.astype(jnp.float32) + attended_rows.astype(jnp.float32)).astype(
        jnp.bfloat16
    )
    scaled, normed, inv_root, queries, keys_low, values_low = project(
        stored_rows, squares(stored_rows), gains_full
    )
    query_heads, key_heads, value_heads, upstream_heads = (
        lax.all_to_all(queries, "seq", split_axis=1, concat_axis=0, tiled=True),
        lax.all_to_all(keys_low, "seq", split_axis=1, concat_axis=0, tiled=True),
        lax.all_to_all(values_low, "seq", split_axis=1, concat_axis=0, tiled=True),
        lax.all_to_all(upstream, "seq", split_axis=1, concat_axis=0, tiled=True),
    )
    query_low, key_low, value_low, bias_part = attend_back(
        query_heads, key_heads, value_heads, upstream_heads, bias_local, sky_backward
    )
    query_rows, key_rows, value_rows = (
        lax.all_to_all(query_low, "seq", split_axis=0, concat_axis=1, tiled=True),
        lax.all_to_all(key_low, "seq", split_axis=0, concat_axis=1, tiled=True),
        lax.all_to_all(value_low, "seq", split_axis=0, concat_axis=1, tiled=True),
    )
    scaled_grad, partials_full, local_mix = tail_start(
        query_rows, key_rows, value_rows, scaled, normed, gains_full
    )
    input_grad = finish(upstream, scaled_grad, scaled, inv_root, local_mix)
    channel_part = lax.psum_scatter(partials_full, "seq", scatter_dimension=1, tiled=True)
    channel_sum, bias_sum = lax.psum((channel_part, bias_part), "dp")
    replicas = lax.axis_size("dp")
    sent_forward = from_behind(section_result, "pipe", 1)
    sent_backward = from_behind(input_grad, "pipe", -1)
    return (
        sent_forward[None, None],
        sent_backward[None, None],
        (channel_sum / replicas)[None],
        (bias_sum / replicas)[None],
    )


def solution(mesh):
    placed = (
        P("pipe", "dp", "seq", None),
        P("pipe", "dp", "seq", None),
        P("pipe", "dp", "seq", None),
        P("pipe", "dp", None),
        P("pipe", "dp", None),
        P("pipe", None),
        P("pipe", None),
        P("pipe", None),
        P("pipe", None),
        P("pipe", None),
    )
    return jax.shard_map(
        on_device,
        mesh=mesh,
        in_specs=placed,
        out_specs=(
            P("pipe", "dp", "seq", None),
            P("pipe", "dp", "seq", None),
            P("pipe", None, "seq"),
            P("pipe", "seq"),
        ),
        check_vma=False,
    )
```

profile of v0, /device:TPU:8, one launch (start us, length us, event | category | flops | bytes accessed | tf_op | source)
XLA Modules:
  0.0 357.5 jit_solution(10406012320160889055)
XLA Ops:
  15.0 28.1 %all_to_all.137 = bf16[128,8,256]{0,2,1:T(8,128)(2,1)S(1)} all-to-all(bf16[128,8,256]{0,2,1:T(8,128)(2,1)S(1)} %get-tuple-element.15), channel_id=1, replica_groups=mesh['dp'=16,'pipe'=8,'seq'=8] {'seq'}, dimensions={1} | all-to-all | bytes 1048576 | tf_op jit(solution)/shard_map/all_to_all | solution.py:188
  43.1 16.3 %all_to_all.138 = bf16[128,8,256]{0,2,1:T(8,128)(2,1)S(1)} all-to-all(bf16[128,8,256]{0,2,1:T(8,128)(2,1)S(1)} %get-tuple-element.14), channel_id=1, replica_groups=mesh['dp'=16,'pipe'=8,'seq'=8] {'seq'}, dimensions={1} | all-to-all | bytes 1048576 | tf_op jit(solution)/shard_map/all_to_all | solution.py:187
  59.3 5.4 %all-to-all-start.6 = ((bf16[128,8,256]{0,2,1:T(8,128)(2,1)}), bf16[128,8,256]{0,2,1:T(8,128)(2,1)S(1)}, u32[]{:S(2)}, u32[]{:S(2)}) async-start(bf16[128,8,256]{0,2,1:T(8,128)(2,1)} %get-tuple-element.13), calls=%async_computation.6 | async-start | bytes 1048576 | tf_op jit(solution)/shard_map/all_to_all | solution.py:189
  66.0 11.1 %all-to-all-done.6 = bf16[128,8,256]{0,2,1:T(8,128)(2,1)S(1)} async-done(((bf16[128,8,256]{0,2,1:T(8,128)(2,1)}), bf16[128,8,256]{0,2,1:T(8,128)(2,1)S(1)}, u32[]{:S(2)}, u32[]{:S(2)}) %all-to-all-start.6) | async-done | bytes 524320 | tf_op jit(solution)/shard_map/all_to_all | solution.py:189
  77.1 6.2 %all-to-all-start.7 = ((bf16[128,8,256]{0,2,1:T(8,128)(2,1)}), bf16[128,8,256]{0,2,1:T(8,128)(2,1)}, u32[]{:S(2)}, u32[]{:S(2)}) async-start(bf16[128,8,256]{0,2,1:T(8,128)(2,1)} %bitcast.29), calls=%async_computation.7 | async-start | bytes 1048576 | tf_op jit(solution)/shard_map/all_to_all | solution.py:190
  86.3 3.3 fusion.103
  89.5 5.8 %all-to-all-done.7 = bf16[128,8,256]{0,2,1:T(8,128)(2,1)} async-done(((bf16[128,8,256]{0,2,1:T(8,128)(2,1)}), bf16[128,8,256]{0,2,1:T(8,128)(2,1)}, u32[]{:S(2)}, u32[]{:S(2)}) %all-to-all-start.7) | async-done | bytes 524320 | tf_op jit(solution)/shard_map/all_to_all | solution.py:190
  100.6 4.7 %all-to-all-start.8 = ((bf16[8,128,256]{1,2,0:T(8,128)(2,1)}), bf16[8,128,256]{1,2,0:T(8,128)(2,1)S(1)}, u32[]{:S(2)}, u32[]{:S(2)}) async-start(bf16[8,128,256]{1,2,0:T(8,128)(2,1)} %bitcast.179), calls=%async_computation.8 | async-start | bytes 1048576 | tf_op jit(solution)/shard_map/all_to_all | solution.py:196
  106.8 15.3 %all-to-all-done.8 = bf16[8,128,256]{1,2,0:T(8,128)(2,1)S(1)} async-done(((bf16[8,128,256]{1,2,0:T(8,128)(2,1)}), bf16[8,128,256]{1,2,0:T(8,128)(2,1)S(1)}, u32[]{:S(2)}, u32[]{:S(2)}) %all-to-all-start.8) | async-done | bytes 524320 | tf_op jit(solution)/shard_map/all_to_all | solution.py:196
  122.1 5.5 %all-to-all-start.9 = ((bf16[8,128,256]{1,2,0:T(8,128)(2,1)}), bf16[8,128,256]{1,2,0:T(8,128)(2,1)S(1)}, u32[]{:S(2)}, u32[]{:S(2)}) async-start(bf16[8,128,256]{1,2,0:T(8,128)(2,1)} %bitcast.40), calls=%async_computation.9 | async-start | bytes 1048576 | tf_op jit(solution)/shard_map/all_to_all | solution.py:197
  130.9 13.3 %all-to-all-done.9 = bf16[8,128,256]{1,2,0:T(8,128)(2,1)S(1)} async-done(((bf16[8,128,256]{1,2,0:T(8,128)(2,1)}), bf16[8,128,256]{1,2,0:T(8,128)(2,1)S(1)}, u32[]{:S(2)}, u32[]{:S(2)}) %all-to-all-start.9) | async-done | bytes 524320 | tf_op jit(solution)/shard_map/all_to_all | solution.py:197
  144.2 4.8 %all-to-all-start.10 = ((bf16[8,128,256]{1,2,0:T(8,128)(2,1)}), bf16[8,128,256]{1,2,0:T(8,128)(2,1)S(1)}, u32[]{:S(2)}, u32[]{:S(2)}) async-start(bf16[8,128,256]{1,2,0:T(8,128)(2,1)} %bitcast.171), calls=%async_computation.10 | async-start | bytes 1048576 | tf_op jit(solution)/shard_map/all_to_all | solution.py:198
  150.5 12.7 %all-to-all-done.10 = bf16[8,128,256]{1,2,0:T(8,128)(2,1)S(1)} async-done(((bf16[8,128,256]{1,2,0:T(8,128)(2,1)}), bf16[8,128,256]{1,2,0:T(8,128)(2,1)S(1)}, u32[]{:S(2)}, u32[]{:S(2)}) %all-to-all-start.10) | async-done | bytes 524320 | tf_op jit(solution)/shard_map/all_to_all | solution.py:198
  163.1 4.7 %multiply_convert_fusion.3 = (bf16[128,8,256]{0,2,1:T(8,128)(2,1)S(1)}, bf16[128,8,256]{0,2,1:T(8,128)(2,1)}, bf16[128,8,256]{0,2,1:T(8,128)(2,1)S(1)}, f32[8,25...) fusion(f32[128,8,256]{0,2,1:T(8,128)} %bitcast.168, ...), kind=kLoop, calls=%fused_computation.80 | loop fusion | flops 7593856 | bytes 5309952 | tf_op jit(solution)/shard_map/convert_element_type | solution.py:27
  167.8 18.9 %all_to_all.139 = bf16[128,8,256]{0,2,1:T(8,128)(2,1)S(1)} all-to-all(bf16[128,8,256]{0,2,1:T(8,128)(2,1)S(1)} %get-tuple-element.16), channel_id=1, replica_groups=mesh['dp'=16,'pipe'=8,'seq'=8] {'seq'}, dimensions={1} | all-to-all | bytes 1048576 | tf_op jit(solution)/shard_map/all_to_all | solution.py:175
  186.7 17.1 %all_to_all.140 = bf16[128,8,256]{0,2,1:T(8,128)(2,1)S(1)} all-to-all(bf16[128,8,256]{0,2,1:T(8,128)(2,1)S(1)} %get-tuple-element.18), channel_id=1, replica_groups=mesh['dp'=16,'pipe'=8,'seq'=8] {'seq'}, dimensions={1} | all-to-all | bytes 1048576 | tf_op jit(solution)/shard_map/all_to_all | solution.py:176
  203.8 5.5 %all-to-all-start.1 = ((bf16[128,8,256]{0,2,1:T(8,128)(2,1)}), bf16[128,8,256]{0,2,1:T(8,128)(2,1)}, u32[]{:S(2)}, u32[]{:S(2)}) async-start(bf16[128,8,256]{0,2,1:T(8,128)(2,1)} %get-tuple-element.17), calls=%async_computation.1 | async-start | bytes 1048576 | tf_op jit(solution)/shard_map/all_to_all | solution.py:174
  213.1 13.1 %all-to-all-done.1 = bf16[128,8,256]{0,2,1:T(8,128)(2,1)} async-done(((bf16[128,8,256]{0,2,1:T(8,128)(2,1)}), bf16[128,8,256]{0,2,1:T(8,128)(2,1)}, u32[]{:S(2)}, u32[]{:S(2)}) %all-to-all-start.1) | async-done | bytes 524320 | tf_op jit(solution)/shard_map/all_to_all | solution.py:174
  226.3 3.5 fusion.106
  229.8 2.9 convolution_convert_fusion
  232.7 6.0 %all-to-all-start.3 = ((bf16[8,128,256]{1,2,0:T(8,128)(2,1)}), bf16[8,128,256]{1,2,0:T(8,128)(2,1)}, u32[]{:S(2)}, u32[]{:S(2)}) async-start(bf16[8,128,256]{1,2,0:T(8,128)(2,1)} %bitcast.13), calls=%async_computation.3 | async-start | bytes 1048576 | tf_op jit(solution)/shard_map/all_to_all | solution.py:179
  243.1 3.2 fusion.31
  255.6 35.5 %reduce-scatter.4.cloned.1.call-done = f32[256,4]{1,0:T(8,128)} async-done(((f32[2048,4]{1,0:T(8,128)}), f32[256,4]{1,0:T(8,128)}) %reduce-scatter.4.cloned.1.call-update) | async-done | bytes 4112
  292.1 55.9 %all-reduce.8 = (f32[4,256]{1,0:T(4,128)S(1)}, f32[2]{0:T(128)S(1)}) all-reduce(f32[4,256]{1,0:T(4,128)S(1)} %copy.67, f32[2]{0:T(128)S(1)} %get-tuple-element.11), channel_id=1, replica_groups=mesh['dp'=16,'pipe'=8,'seq'=8] {'dp'}, use_global_device_ids=true, to_apply=%region_13.14 | all-reduce | flops 1026 | bytes 8208 | tf_op jit(solution)/shard_map/psum | solution.py:205
  (113 shorter events, 44.3 us)
Async XLA Ops:
  7.2 76.1 %copy-start = (f32[1,16]{1,0:T(1,128)S(1)}, f32[1,16]{1,0:T(1,128)}, u32[]{:S(2)}) copy-start(f32[1,16]{1,0:T(1,128)} %param.19) | copy-start | bytes 196
  7.2 3.1 copy-start.13
  7.2 3.7 %copy-start.15 = (f32[1,2048]{1,0:T(1,128)S(1)}, f32[1,2048]{1,0:T(1,128)}, u32[]{:S(2)}) copy-start(f32[1,2048]{1,0:T(1,128)} %param.18) | copy-start | bytes 24580
  7.2 4.4 %copy-start.14 = (f32[1,2048]{1,0:T(1,128)S(1)}, f32[1,2048]{1,0:T(1,128)}, u32[]{:S(2)}) copy-start(f32[1,2048]{1,0:T(1,128)} %param.16) | copy-start | bytes 24580
  7.2 5.1 %copy-start.12 = (f32[1,2048]{1,0:T(1,128)S(1)}, f32[1,2048]{1,0:T(1,128)}, u32[]{:S(2)}) copy-start(f32[1,2048]{1,0:T(1,128)} %param.17) | copy-start | bytes 24580
  15.0 49.7 %copy-start.16 = (s32[1,1,1024]{2,1,0:T(1,128)S(1)}, s32[1,1,1024]{2,1,0:T(1,128)}, u32[]{:S(2)}) copy-start(s32[1,1,1024]{2,1,0:T(1,128)} %param.13) | copy-start | bytes 12292
  15.0 49.8 %copy-start.17 = (s32[1,1,1024]{2,1,0:T(1,128)S(1)}, s32[1,1,1024]{2,1,0:T(1,128)}, u32[]{:S(2)}) copy-start(s32[1,1,1024]{2,1,0:T(1,128)} %param.14) | copy-start | bytes 12292
  15.0 49.8 %copy-start.6 = (bf16[1,1,128,2048]{3,2,1,0:T(8,128)(2,1)S(1)}, bf16[1,1,128,2048]{3,2,1,0:T(8,128)(2,1)}, u32[]{:S(2)}) copy-start(bf16[1,1,128,2048]{3,2,1,0:T(8,128)(2,1)} %param.12) | copy-start | bytes 1572868
  59.3 26.9 %copy-start.3 = (bf16[128,8,256]{0,2,1:T(8,128)(2,1)}, bf16[128,8,256]{0,2,1:T(8,128)(2,1)S(1)}, u32[]{:S(2)}) copy-start(bf16[128,8,256]{0,2,1:T(8,128)(2,1)S(1)} %all_to_all.138) | copy-start | bytes 1572868
  59.3 17.7 %all-to-all-start.6 = ((bf16[128,8,256]{0,2,1:T(8,128)(2,1)}), bf16[128,8,256]{0,2,1:T(8,128)(2,1)S(1)}, u32[]{:S(2)}, u32[]{:S(2)}) async-start(bf16[128,8,256]{0,2,1:T(8,128)(2,1)} %get-tuple-element.13), calls=%async_computation.6 | async-start | bytes 1048576 | tf_op jit(solution)/shard_map/all_to_all | solution.py:189
  77.1 18.2 %all-to-all-start.7 = ((bf16[128,8,256]{0,2,1:T(8,128)(2,1)}), bf16[128,8,256]{0,2,1:T(8,128)(2,1)}, u32[]{:S(2)}, u32[]{:S(2)}) async-start(bf16[128,8,256]{0,2,1:T(8,128)(2,1)} %bitcast.29), calls=%async_computation.7 | async-start | bytes 1048576 | tf_op jit(solution)/shard_map/all_to_all | solution.py:190
  84.9 4.6 %copy-start.8 = (bf16[8,128,2,128]{3,1,2,0:T(8,128)(2,1)}, bf16[8,128,2,128]{3,1,2,0:T(8,128)(2,1)S(1)}, u32[]{:S(2)}) copy-start(bf16[8,128,2,128]{3,1,2,0:T(8,128)(2,1)S(1)} %copy.49) | copy-start | bytes 1572868
  86.2 9.1 %copy-start.11 = (bf16[7,128,2,128]{3,1,2,0:T(8,128)(2,1)S(1)}, bf16[7,128,2,128]{3,1,2,0:T(8,128)(2,1)}, u32[]{:S(2)}) copy-start(bf16[7,128,2,128]{3,1,2,0:T(8,128)(2,1)} %copy.51) | copy-start | bytes 1376260
  95.3 2.8 copy-start.5
  99.3 6.0 %copy-start.4 = (bf16[128,8,256]{0,2,1:T(8,128)(2,1)S(1)}, bf16[128,8,256]{0,2,1:T(8,128)(2,1)}, u32[]{:S(2)}) copy-start(bf16[128,8,256]{0,2,1:T(8,128)(2,1)} %copy-done.3) | copy-start | bytes 1572868
  100.6 21.5 %all-to-all-start.8 = ((bf16[8,128,256]{1,2,0:T(8,128)(2,1)}), bf16[8,128,256]{1,2,0:T(8,128)(2,1)S(1)}, u32[]{:S(2)}, u32[]{:S(2)}) async-start(bf16[8,128,256]{1,2,0:T(8,128)(2,1)} %bitcast.179), calls=%async_computation.8 | async-start | bytes 1048576 | tf_op jit(solution)/shard_map/all_to_all | solution.py:196
  122.1 22.1 %all-to-all-start.9 = ((bf16[8,128,256]{1,2,0:T(8,128)(2,1)}), bf16[8,128,256]{1,2,0:T(8,128)(2,1)S(1)}, u32[]{:S(2)}, u32[]{:S(2)}) async-start(bf16[8,128,256]{1,2,0:T(8,128)(2,1)} %bitcast.40), calls=%async_computation.9 | async-start | bytes 1048576 | tf_op jit(solution)/shard_map/all_to_all | solution.py:197
  130.0 19.1 %copy-start.1 = (bf16[1,1,128,2048]{3,2,1,0:T(8,128)(2,1)S(1)}, bf16[1,1,128,2048]{3,2,1,0:T(8,128)(2,1)}, u32[]{:S(2)}) copy-start(bf16[1,1,128,2048]{3,2,1,0:T(8,128)(2,1)} %param.10) | copy-start | bytes 1572868
  144.2 18.9 %all-to-all-start.10 = ((bf16[8,128,256]{1,2,0:T(8,128)(2,1)}), bf16[8,128,256]{1,2,0:T(8,128)(2,1)S(1)}, u32[]{:S(2)}, u32[]{:S(2)}) async-start(bf16[8,128,256]{1,2,0:T(8,128)(2,1)} %bitcast.171), calls=%async_computation.10 | async-start | bytes 1048576 | tf_op jit(solution)/shard_map/all_to_all | solution.py:198
  203.8 22.5 %all-to-all-start.1 = ((bf16[128,8,256]{0,2,1:T(8,128)(2,1)}), bf16[128,8,256]{0,2,1:T(8,128)(2,1)}, u32[]{:S(2)}, u32[]{:S(2)}) async-start(bf16[128,8,256]{0,2,1:T(8,128)(2,1)} %get-tuple-element.17), calls=%async_computation.1 | async-start | bytes 1048576 | tf_op jit(solution)/shard_map/all_to_all | solution.py:174
  232.7 18.0 %all-to-all-start.3 = ((bf16[8,128,256]{1,2,0:T(8,128)(2,1)}), bf16[8,128,256]{1,2,0:T(8,128)(2,1)}, u32[]{:S(2)}, u32[]{:S(2)}) async-start(bf16[8,128,256]{1,2,0:T(8,128)(2,1)} %bitcast.13), calls=%async_computation.3 | async-start | bytes 1048576 | tf_op jit(solution)/shard_map/all_to_all | solution.py:179
  238.7 52.4 %reduce-scatter.4.cloned.1.call-start = ((), (), s32[]{:S(2)}) async-start(), calls=%async_computation.12 | async-start | bytes 1179648
  246.3 102.8 %collective-permute-start.1 = (bf16[128,2048]{1,0:T(8,128)(2,1)}, bf16[128,2048]{1,0:T(8,128)(2,1)S(1)}, u32[]{:S(2)}, u32[]{:S(2)}) collective-permute-start(bf16[128,2048]{1,0:T(8,128)(2,1)} %fusion.31), channel_id=1, source_target_pairs={{0,56},{8,0},{16,8},{24,16},{32,24},{40,32},{48,40},{56,48},{1,57}... | collective-permute-start | bytes 1572872 | tf_op jit(solution)/shard_map/ppermute | solution.py:17
  252.3 96.8 %collective-permute-start = (bf16[128,2048]{1,0:T(8,128)(2,1)S(1)}, bf16[128,2048]{1,0:T(8,128)(2,1)S(1)}, u32[]{:S(2)}, u32[]{:S(2)}) collective-permute-start(bf16[128,2048]{1,0:T(8,128)(2,1)S(1)} %fusion.42), channel_id=1, source_target_pairs={{0,8},{8,16},{16,24},{24,32},{32,40},{40,48},{48,56},{56,0},{1,9},... | collective-permute-start | bytes 1572872 | tf_op jit(solution)/shard_map/ppermute | solution.py:17
  (4 other events, 5.0 us)
Sparse Core Ops, SparseCore 0:
  255.7 35.2 reduce-scatter.3
where the time goes:
time: 359 us; the launch traced here: 357 us
  blocking collectives  136 us (38%)
  waiting for transfers between devices  109 us (30%)
  starting transfers between devices  42 us (12%)
  other arithmetic  19.9 us (6%)
  local copies, waits for them, and re-layouts  19.2 us (5%)
  matrix products  16.5 us (5%)
  between operations  14.5 us (4%)
    psum x1, blocking collectives, on_device(): channel_sum, bias_sum = lax.psum((channel_part, bias_part), 'dp')  55.9 us
    all_to_all x2, blocking collectives, on_device(): lax.all_to_all(keys_low, 'seq', split_axis=1, concat_axis=0, tiled=True)  47 us
    unnamed x2, waiting for transfers between devices  35.5 us
    all_to_all x1, blocking collectives, on_device(): lax.all_to_all(values_low, 'seq', split_axis=1, concat_axis=0, tiled=True)  17.1 us
    all_to_all x1, blocking collectives, on_device(): lax.all_to_all(queries, 'seq', split_axis=1, concat_axis=0, tiled=True)  16.3 us
    all_to_all x1, waiting for transfers between devices, on_device(): lax.all_to_all(query_low, 'seq', split_axis=0, concat_axis=1, tiled=True)  15.3 us
    all_to_all x1, waiting for transfers between devices, on_device(): lax.all_to_all(key_low, 'seq', split_axis=0, concat_axis=1, tiled=True)  13.3 us
    all_to_all x1, waiting for transfers between devices, on_device(): lax.all_to_all(queries, 'seq', split_axis=1, concat_axis=0, tiled=True)  13.1 us
  transfers between devices with their start and end apart: 10, of which 8 were waited for; matrix products, arithmetic and copies ran while one was open for 8% of the time, Pallas kernels for 0%

commit v1 on v0

v1 whole, which is shorter than its diff:
```python
import functools
import math

import jax
import jax.numpy as jnp
from jax import lax
from jax.experimental import pallas as pl
from jax.experimental.pallas import tpu as pltpu
from jax.sharding import PartitionSpec as P

D = 2048
HEAD_DIM = 128
BATCH = 16
BLOCK = 128
WIDE = 256
CHUNKS = D // WIDE
AHEAD = 3

epsilon = 1e-05
factor = 1.0 / math.sqrt(HEAD_DIM)
f32 = jnp.float32
bf16 = jnp.bfloat16
MESH = pl.DeviceIdType.MESH


def dot(a, b, contract):
    return lax.dot_general(a, b, ((contract[:1], contract[1:]), ((), ())), preferred_element_type=f32)


def column_of(row):
    return jnp.transpose(jnp.broadcast_to(row, (BLOCK, BLOCK)))


def twice(square):
    return jnp.concatenate([square, square], axis=1)


def kernel(
    sizes,
    fx_ref, sx_ref, og_ref, fsky_ref, bsky_ref, ng_ref, qs_ref, ks_ref, vs_ref, bias_ref,
    fo_ref, bo_ref, sg_ref, bg_ref,
    sx, og, fx, halo, crecv, csend, bsend, fsend, grads,
    ng, qs, ks, vs, fsky, bsky,
    inv_s, inv_f, inv_sp, inv_fp, sky_s, sky_f, mask,
    stat_send, stat_recv, part_send, part_recv, xs, zs, zr,
    load_sem, x_send, x_recv, c_send, c_recv, stat_sem, p_send, p_recv,
    xs_send, xs_recv, z_send, z_recv, fo_send, fo_recv, bo_send, bo_recv,
):
    n_dp, n_pipe, n_seq = sizes
    me = lax.axis_index("seq")
    pipe = lax.axis_index("pipe")
    dp = lax.axis_index("dp")
    nxt, prv = lax.rem(me + 1, n_seq), lax.rem(me + n_seq - 1, n_seq)
    pnext, pprev = lax.rem(pipe + 1, n_pipe), lax.rem(pipe + n_pipe - 1, n_pipe)
    zi, xi = dp // 4, lax.rem(dp, 4)
    x_peers = [zi * 4 + lax.rem(xi + d, 4) for d in (1, 2, 3)]
    z_peers = [(zi + 1 - 2 * lax.rem(zi, 2)) * 4 + xi, (3 - zi) * 4 + xi]

    barrier = pltpu.get_barrier_semaphore()
    greeted = [{"seq": lax.rem(me + d, n_seq)} for d in range(1, n_seq)]
    greeted += [{"pipe": pnext}, {"pipe": pprev}]
    if n_dp == 16:
        greeted += [{"dp": peer} for peer in x_peers + z_peers]
    for peer in greeted:
        pl.semaphore_signal(barrier, inc=1, device_id=peer, device_id_type=MESH)

    def columns(c):
        return pl.ds(pl.multiple_of(c * WIDE, WIDE), WIDE)

    loads = []
    for source, target in ((sx_ref, sx), (fx_ref, fx), (og_ref, og)):
        for c in range(CHUNKS):
            loads.append((source.at[:, c * WIDE : (c + 1) * WIDE], target.at[c]))
    for source, target in (
        (ng_ref, ng), (qs_ref, qs), (ks_ref, ks), (vs_ref, vs), (fsky_ref, fsky), (bsky_ref, bsky),
    ):
        loads.append((source, target))
    copies = [pltpu.make_async_copy(a, b, load_sem.at[i]) for i, (a, b) in enumerate(loads)]
    for copy in copies:
        copy.start()

    def halo_copy(source, c, slot):
        return pltpu.make_async_remote_copy(
            src_ref=source.at[:, columns(c)],
            dst_ref=halo.at[slot],
            send_sem=x_send.at[slot],
            recv_sem=x_recv.at[slot],
            device_id={"seq": nxt},
            device_id_type=MESH,
        )

    def saved_halo(c):
        return halo_copy(sx_ref, c, c)

    def forward_halo(c):
        return halo_copy(fx_ref, c, c + CHUNKS)

    pl.semaphore_wait(barrier, len(greeted))
    for c in range(AHEAD - 1):
        saved_halo(c).start()

    def inverse_root(target):
        def add(c, total):
            rows = target[c].astype(f32)
            return total + rows * rows

        total = lax.fori_loop(0, CHUNKS, add, jnp.zeros((BLOCK, WIDE), f32))
        return lax.rsqrt(jnp.sum(total, axis=1, keepdims=True) / D + epsilon)

    for copy in copies[:CHUNKS]:
        copy.wait()
    inv = jnp.broadcast_to(inverse_root(sx), (BLOCK, BLOCK))
    inv_s[...] = twice(inv)
    stat_send[0:4, :] = jnp.transpose(inv)[0:4, :]
    for copy in copies[CHUNKS : 2 * CHUNKS]:
        copy.wait()
    inv = jnp.broadcast_to(inverse_root(fx), (BLOCK, BLOCK))
    inv_f[...] = twice(inv)
    stat_send[4:8, :] = jnp.transpose(inv)[0:4, :]
    stat_copy = pltpu.make_async_remote_copy(
        src_ref=stat_send,
        dst_ref=stat_recv,
        send_sem=stat_sem.at[0],
        recv_sem=stat_sem.at[1],
        device_id={"seq": nxt},
        device_id_type=MESH,
    )
    stat_copy.start()
    saved_halo(AHEAD - 1).start()

    for copy in copies[2 * CHUNKS :]:
        copy.wait()

    for source, target in ((bsky, sky_s), (fsky, sky_f)):
        for half, block in ((0, prv), (1, me)):
            row = source[:, pl.ds(pl.multiple_of(block * BLOCK, BLOCK), BLOCK)].astype(f32)
            target[half * BLOCK : (half + 1) * BLOCK, :] = column_of(row)
    outer = lax.broadcasted_iota(jnp.int32, (2 * BLOCK, BLOCK), 0)
    inner = lax.broadcasted_iota(jnp.int32, (2 * BLOCK, BLOCK), 1)
    first_key = jnp.where(me > 0, 0, BLOCK)
    inside = (outer > inner) & (outer <= inner + BLOCK) & (outer >= first_key)
    mask[...] = jnp.where(inside, 0.0, -1e30).astype(f32)

    stat_copy.wait_recv()
    inv_sp[...] = twice(column_of(stat_recv[0:1, :]))
    inv_fp[...] = twice(column_of(stat_recv[4:5, :]))

    def gains_of(c):
        return tuple(r[:, columns(c)] for r in (ng, qs, ks, vs))

    def probabilities(key_window, query, head, sky):
        scores = dot(key_window, query, (1, 1)) * factor
        scores = scores + (bias_ref[0, head] * sky[...] + mask[...])
        top = jnp.max(scores, axis=0, keepdims=True)
        raised = jnp.exp(scores - top)
        return raised * (1.0 / jnp.sum(raised, axis=0, keepdims=True))

    def part_copy(c, slot, peer):
        return pltpu.make_async_remote_copy(
            src_ref=part_send.at[c],
            dst_ref=part_recv.at[slot],
            send_sem=p_send.at[c],
            recv_sem=p_recv.at[slot],
            device_id={"seq": peer},
            device_id_type=MESH,
        )

    def fold_copy(c):
        return pltpu.make_async_remote_copy(
            src_ref=csend.at[c],
            dst_ref=crecv.at[c],
            send_sem=c_send.at[c],
            recv_sem=c_recv.at[c],
            device_id={"seq": prv},
            device_id_type=MESH,
        )

    def backward_chunk(c, carry):
        saved_halo(c).wait_recv()
        gain, query_s, key_s, value_s = gains_of(c)
        scaled = sx[c].astype(f32) * inv_s[...]
        normed = scaled * gain
        query = (normed * query_s).astype(bf16)
        key = (normed * key_s).astype(bf16)
        value = (normed * value_s).astype(bf16)
        scaled_p = halo[c].astype(f32) * inv_sp[...]
        normed_p = scaled_p * gain
        key_p = (normed_p * key_s).astype(bf16)
        value_p = (normed_p * value_s).astype(bf16)
        upstream = og[c]
        query_grads, key_grads, value_grads, biases = [], [], [], []
        for h in range(2):
            s = slice(h * HEAD_DIM, (h + 1) * HEAD_DIM)
            query_h, upstream_h = query[:, s], upstream[:, s]
            key_window = jnp.concatenate([key_p[:, s], key[:, s]], axis=0)
            value_window = jnp.concatenate([value_p[:, s], value[:, s]], axis=0)
            probs = probabilities(key_window, query_h, 2 * c + h, sky_s)
            value_grads.append(dot(probs.astype(bf16), upstream_h, (1, 0)))
            prob_grad = dot(value_window, upstream_h, (1, 1))
            score_grad = probs * (prob_grad - jnp.sum(probs * prob_grad, axis=0, keepdims=True))
            biases.append(jnp.sum(score_grad * sky_s[...], axis=0, keepdims=True))
            score_low = score_grad.astype(bf16)
            key_grads.append(dot(score_low, query_h, (1, 0)) * factor)
            query_grads.append(dot(score_low, key_window, (0, 0)) * factor)
        query_grad = jnp.concatenate(query_grads, axis=1).astype(bf16).astype(f32)
        key_grad = jnp.concatenate(key_grads, axis=1)
        value_grad = jnp.concatenate(value_grads, axis=1)
        key_b, key_a = key_grad[:BLOCK], key_grad[BLOCK:]
        value_b, value_a = value_grad[:BLOCK], value_grad[BLOCK:]
        csend[c] = (key_b * key_s + value_b * value_s).astype(bf16)
        fold_copy(c).start()
        grads[c] = query_grad * query_s + key_a * key_s + value_a * value_s
        sums = (
            jnp.sum(query_grad * scaled, axis=0, keepdims=True),
            jnp.sum(key_a * scaled + key_b * scaled_p, axis=0, keepdims=True),
            jnp.sum(value_a * scaled + value_b * scaled_p, axis=0, keepdims=True),
        )
        for i, row in enumerate(sums):
            part_send[c, 2 * i : 2 * i + 1, :] = row[:, :HEAD_DIM]
            part_send[c, 2 * i + 1 : 2 * i + 2, :] = row[:, HEAD_DIM:]
        part_send[c, 6:7, :] = biases[0]
        part_send[c, 7:8, :] = biases[1]

        @pl.when(c != me)
        def _():
            part_copy(c, me, c).start()

        @pl.when(c < CHUNKS - AHEAD)
        def _():
            saved_halo(c + AHEAD).start()

        @pl.when(c >= CHUNKS - AHEAD)
        def _():
            forward_halo(c + AHEAD - CHUNKS).start()

        return carry

    lax.fori_loop(0, CHUNKS, backward_chunk, 0)

    def start_forward_halo(c, carry):
        forward_halo(c).start()
        return carry

    lax.fori_loop(AHEAD, CHUNKS, start_forward_halo, 0)

    def fold(c, total):
        fold_copy(c).wait_recv()
        scaled_grad = (grads[c] + crecv[c].astype(f32)) * ng[:, columns(c)]
        grads[c] = scaled_grad
        return total + scaled_grad * (sx[c].astype(f32) * inv_s[...])

    total = lax.fori_loop(0, CHUNKS, fold, jnp.zeros((BLOCK, WIDE), f32))
    mean = jnp.broadcast_to(jnp.sum(total, axis=1, keepdims=True) / D, (BLOCK, WIDE))

    def bwd_copy(c):
        return pltpu.make_async_remote_copy(
            src_ref=bsend.at[c],
            dst_ref=bo_ref.at[:, columns(c)],
            send_sem=bo_send.at[c],
            recv_sem=bo_recv.at[c],
            device_id={"pipe": pprev},
            device_id_type=MESH,
        )

    def finish(c, carry):
        root = inv_s[...]
        scaled = sx[c].astype(f32) * root
        bsend[c] = (og[c].astype(f32) + root * (grads[c] - scaled * carry)).astype(bf16)
        bwd_copy(c).start()
        return carry

    lax.fori_loop(0, CHUNKS, finish, mean)

    def fwd_copy(c):
        return pltpu.make_async_remote_copy(
            src_ref=fsend.at[c],
            dst_ref=fo_ref.at[:, columns(c)],
            send_sem=fo_send.at[c],
            recv_sem=fo_recv.at[c],
            device_id={"pipe": pnext},
            device_id_type=MESH,
        )

    def forward_chunk(c, carry):
        forward_halo(c).wait_recv()
        gain, query_s, key_s, value_s = gains_of(c)
        rows = fx[c].astype(f32)
        normed = rows * inv_f[...] * gain
        query = (normed * query_s).astype(bf16)
        key = (normed * key_s).astype(bf16)
        value = (normed * value_s).astype(bf16)
        normed_p = halo[c + CHUNKS].astype(f32) * inv_fp[...] * gain
        key_p = (normed_p * key_s).astype(bf16)
        value_p = (normed_p * value_s).astype(bf16)
        attended = []
        for h in range(2):
            s = slice(h * HEAD_DIM, (h + 1) * HEAD_DIM)
            key_window = jnp.concatenate([key_p[:, s], key[:, s]], axis=0)
            value_window = jnp.concatenate([value_p[:, s], value[:, s]], axis=0)
            probs = probabilities(key_window, query[:, s], 2 * c + h, sky_f).astype(bf16)
            attended.append(dot(probs, value_window, (0, 0)))
        attended = jnp.concatenate(attended, axis=1).astype(bf16).astype(f32)
        fsend[c] = (rows + attended).astype(bf16)
        fwd_copy(c).start()
        return carry

    def seq_sum():
        total = part_send[me]
        for d in range(1, n_seq):
            peer = lax.rem(me + d, n_seq)
            part_copy(peer, peer, peer).wait_recv()
            total = total + part_recv[peer]
        return total

    def x_copy(i):
        return pltpu.make_async_remote_copy(
            src_ref=xs.at[xi],
            dst_ref=xs.at[xi],
            send_sem=xs_send.at[i],
            recv_sem=xs_recv.at[xi],
            device_id={"dp": x_peers[i]},
            device_id_type=MESH,
        )

    def x_arrival(i):
        slot = lax.rem(xi + i + 1, 4)
        return pltpu.make_async_remote_copy(
            src_ref=xs.at[slot],
            dst_ref=xs.at[slot],
            send_sem=xs_send.at[i],
            recv_sem=xs_recv.at[slot],
            device_id={"dp": x_peers[i]},
            device_id_type=MESH,
        )

    def z_copy(i):
        return pltpu.make_async_remote_copy(
            src_ref=zs.at[i],
            dst_ref=zr.at[i],
            send_sem=z_send.at[i],
            recv_sem=z_recv.at[i],
            device_id={"dp": z_peers[i]},
            device_id_type=MESH,
        )

    lax.fori_loop(0, 3, forward_chunk, 0)
    total = seq_sum()
    if n_dp == 16:
        xs[xi] = total
        for i in range(3):
            x_copy(i).start()
    lax.fori_loop(3, 5, forward_chunk, 0)
    if n_dp == 16:
        for i in range(3):
            x_arrival(i).wait_recv()
        zs[0] = (xs[0] + xs[1]) + (xs[2] + xs[3])
        z_copy(0).start()
    lax.fori_loop(5, CHUNKS - 1, forward_chunk, 0)
    if n_dp == 16:
        z_copy(0).wait_recv()
        zs[1] = zs[0] + zr[0]
        z_copy(1).start()
    lax.fori_loop(CHUNKS - 1, CHUNKS, forward_chunk, 0)
    if n_dp == 16:
        z_copy(1).wait_recv()
        total = zs[1] + zr[1]

    total = total * (1.0 / BATCH)
    gain, query_s, key_s, value_s = gains_of(me)
    for h in range(2):
        s = slice(h * HEAD_DIM, (h + 1) * HEAD_DIM)
        query_sum, key_sum, value_sum = (total[2 * i + h : 2 * i + h + 1, :] for i in range(3))
        sg_ref[0:1, s] = query_sum * query_s[:, s] + key_sum * key_s[:, s] + value_sum * value_s[:, s]
        sg_ref[1:2, s] = query_sum * gain[:, s]
        sg_ref[2:3, s] = key_sum * gain[:, s]
        sg_ref[3:4, s] = value_sum * gain[:, s]
        bg_ref[0:1, h : h + 1] = jnp.sum(total[6 + h : 7 + h, :], axis=1, keepdims=True)

    stat_copy.wait_send()
    if n_dp == 16:
        for i in range(3):
            x_copy(i).wait_send()
        for i in range(2):
            z_copy(i).wait_send()
    for d in range(1, n_seq):
        peer = lax.rem(me + d, n_seq)
        part_copy(peer, peer, peer).wait_send()

    def drain(c, carry):
        saved_halo(c).wait_send()
        forward_halo(c).wait_send()
        fold_copy(c).wait_send()
        bwd_copy(c).wait()
        fwd_copy(c).wait()
        return carry

    lax.fori_loop(0, CHUNKS, drain, 0)


def solution(mesh):
    sizes = tuple(mesh.shape[name] for name in ("dp", "pipe", "seq"))
    rows = (BLOCK, D)

    def on_device(fwd_input, saved_input, out_grad, fwd_sky, bwd_sky, norm_gain, query_scale, key_scale, value_scale, sky_bias):
        hbm = pl.BlockSpec(memory_space=pltpu.MemorySpace.HBM)
        vmem = pl.BlockSpec(memory_space=pltpu.MemorySpace.VMEM)
        smem = pl.BlockSpec(memory_space=pltpu.MemorySpace.SMEM)
        chunked = pltpu.VMEM((CHUNKS, BLOCK, WIDE), bf16)
        wide = pltpu.VMEM((BLOCK, WIDE), f32)
        window = pltpu.VMEM((2 * BLOCK, BLOCK), f32)
        tile = (8, 128)
        sem = pltpu.SemaphoreType.DMA
        fo, bo, sg, bg = pl.pallas_call(
            functools.partial(kernel, sizes),
            out_shape=(
                jax.ShapeDtypeStruct(rows, bf16),
                jax.ShapeDtypeStruct(rows, bf16),
                jax.ShapeDtypeStruct((4, WIDE), f32),
                jax.ShapeDtypeStruct((1, 2), f32),
            ),
            in_specs=[hbm] * 9 + [smem],
            out_specs=(hbm, hbm, vmem, vmem),
            scratch_shapes=[
                chunked, chunked, chunked,
                pltpu.VMEM((2 * CHUNKS, BLOCK, WIDE), bf16),
                chunked, chunked, chunked, chunked,
                pltpu.VMEM((CHUNKS, BLOCK, WIDE), f32),
                pltpu.VMEM((1, D), f32), pltpu.VMEM((1, D), f32), pltpu.VMEM((1, D), f32), pltpu.VMEM((1, D), f32),
                pltpu.VMEM((1, D // 2), jnp.int32), pltpu.VMEM((1, D // 2), jnp.int32),
                wide, wide, wide, wide, window, window, window,
                pltpu.VMEM(tile, f32), pltpu.VMEM(tile, f32),
                pltpu.VMEM((CHUNKS,) + tile, f32), pltpu.VMEM((CHUNKS,) + tile, f32),
                pltpu.VMEM((4,) + tile, f32), pltpu.VMEM((2,) + tile, f32), pltpu.VMEM((2,) + tile, f32),
                sem((3 * CHUNKS + 6,)), sem((2 * CHUNKS,)), sem((2 * CHUNKS,)), sem((CHUNKS,)), sem((CHUNKS,)),
                sem((2,)), sem((CHUNKS,)), sem((CHUNKS,)),
                sem((3,)), sem((4,)), sem((2,)), sem((2,)),
                sem((CHUNKS,)), sem((CHUNKS,)), sem((CHUNKS,)), sem((CHUNKS,)),
            ],
            compiler_params=pltpu.CompilerParams(collective_id=0, has_side_effects=True),
            name="relay_tick",
        )(
            fwd_input.reshape(rows), saved_input.reshape(rows), out_grad.reshape(rows),
            fwd_sky.reshape(1, -1), bwd_sky.reshape(1, -1),
            norm_gain, query_scale, key_scale, value_scale, sky_bias,
        )
        return fo[None, None], bo[None, None], sg[None], bg

    placed = (
        P("pipe", "dp", "seq", None),
        P("pipe", "dp", "seq", None),
        P("pipe", "dp", "seq", None),
        P("pipe", "dp", None),
        P("pipe", "dp", None),
        P("pipe", None),
        P("pipe", None),
        P("pipe", None),
        P("pipe", None),
        P("pipe", None),
    )
    return jax.shard_map(
        on_device,
        mesh=mesh,
        in_specs=placed,
        out_specs=(
            P("pipe", "dp", "seq", None),
            P("pipe", "dp", "seq", None),
            P("pipe", None, "seq"),
            P("pipe", "seq"),
        ),
        check_vma=False,
    )
```

time: 359 us -> 66 us (0.18)
  the two profiles are of different devices: /device:TPU:8 before, /device:TPU:6 now
where the time goes in v1:
time: 66 us; the launch traced here: 65.8 us
  Pallas kernels  61.3 us (93%)
  local copies, waits for them, and re-layouts  3.91 us (6%)
    pallas_call x1, Pallas kernels, on_device(): pl.pallas_call(functools.partial(kernel, sizes), out_shape=(jax.ShapeDtyp...  61.3 us
    unnamed x10, local copies, waits for them, and re-layouts  3.91 us

profile of v1, /device:TPU:6, one launch (start us, length us, event | category | flops | bytes accessed | tf_op | source)
XLA Modules:
  0.0 65.8 jit_solution(10928590774823673833)
XLA Ops:
  0.6 61.3 %relay_tick.1 = (bf16[128,2048]{1,0:T(8,128)(2,1)}, bf16[128,2048]{1,0:T(8,128)(2,1)}, f32[4,256]{1,0:T(4,128)}, f32[1,2]{1,0:T(1,128)}) custom-call(bf16[128,2048]{1,0:T(8,128)(2,1)} %bitcast.8, bf16[128,2048]{1,0:T(8,128)(2,1)} %bitcast.9, bf16[128,2048]{1,0:T(8,128)(2,1)} %bitcast.10, s32[1,1024]{1,0:T(1,128)} %bitcast.13, s32[1,1024]{1,0:T(1,128)} %bitcast.14, ...), custom_call_target="tpu_custom_call" | custom-call | tf_op jit(solution)/shard_map/relay_tick/pallas_call | solution.py:413
  61.9 0.0 copy-start
  61.9 1.9 %copy.18 = bf16[1,1,128,2048]{3,2,1,0:T(8,128)(2,1)} copy(bf16[1,1,128,2048]{3,2,1,0:T(8,128)(2,1)} %bitcast.12) | data formatting | bytes 1048576
  63.9 0.0 copy-done
  63.9 0.0 copy-start.1
  63.9 0.8 %copy.19 = bf16[1,1,128,2048]{3,2,1,0:T(8,128)(2,1)} copy(bf16[1,1,128,2048]{3,2,1,0:T(8,128)(2,1)S(1)} %bitcast.11) | data formatting | bytes 1048576
  64.7 0.0 copy-done.1
  64.7 0.0 copy-start.2
  64.7 0.6 copy.20
  65.3 0.1 copy-done.2
  65.3 0.5 copy.21
Async XLA Ops:
  61.9 2.0 %copy-start = (bf16[128,2048]{1,0:T(8,128)(2,1)S(1)}, bf16[128,2048]{1,0:T(8,128)(2,1)}, u32[]{:S(2)}) copy-start(bf16[128,2048]{1,0:T(8,128)(2,1)} %get-tuple-element.9) | copy-start | bytes 1572868
  63.9 0.8 %copy-start.1 = (f32[4,256]{1,0:T(4,128)S(1)}, f32[4,256]{1,0:T(4,128)}, u32[]{:S(2)}) copy-start(f32[4,256]{1,0:T(4,128)} %get-tuple-element.10) | copy-start | bytes 12292
  64.7 0.7 %copy-start.2 = (f32[1,2]{1,0:T(1,128)S(1)}, f32[1,2]{1,0:T(1,128)}, u32[]{:S(2)}) copy-start(f32[1,2]{1,0:T(1,128)} %get-tuple-element.19) | copy-start | bytes 28

commit v2 on v1

--- a/solution.py
+++ b/solution.py
@@ -14,7 +14,7 @@
 BLOCK = 128
 WIDE = 256
 CHUNKS = D // WIDE
-AHEAD = 3
+AHEAD = 2
 
 epsilon = 1e-05
 factor = 1.0 / math.sqrt(HEAD_DIM)
@@ -42,9 +42,9 @@
     sx, og, fx, halo, crecv, csend, bsend, fsend, grads,
     ng, qs, ks, vs, fsky, bsky,
     inv_s, inv_f, inv_sp, inv_fp, sky_s, sky_f, mask,
-    stat_send, stat_recv, part_send, part_recv, xs, zs, zr,
+    stat_send, stat_recv, part_send, part_recv, xs, zs,
     load_sem, x_send, x_recv, c_send, c_recv, stat_sem, p_send, p_recv,
-    xs_send, xs_recv, z_send, z_recv, fo_send, fo_recv, bo_send, bo_recv,
+    xs_send, xs_recv, z_send, z_recv, fo_send, fo_recv, bo_send, bo_recv, hello,
 ):
     n_dp, n_pipe, n_seq = sizes
     me = lax.axis_index("seq")
@@ -53,16 +53,41 @@
     nxt, prv = lax.rem(me + 1, n_seq), lax.rem(me + n_seq - 1, n_seq)
     pnext, pprev = lax.rem(pipe + 1, n_pipe), lax.rem(pipe + n_pipe - 1, n_pipe)
     zi, xi = dp // 4, lax.rem(dp, 4)
-    x_peers = [zi * 4 + lax.rem(xi + d, 4) for d in (1, 2, 3)]
-    z_peers = [(zi + 1 - 2 * lax.rem(zi, 2)) * 4 + xi, (3 - zi) * 4 + xi]
+
+    def ring_rank(i, n):
+        return jnp.minimum(i, n - i) * n + i
+
+    groups = [[], [], [], []]
+    for d in range(2, n_seq - 1):
+        peer = lax.rem(me + d, n_seq)
+        groups[0].append((ring_rank(peer, n_seq), ring_rank(me, n_seq), {"seq": peer}))
+    if n_dp == 16:
+        for d in (1, 2, 3):
+            peer = lax.rem(xi + d, 4)
+            groups[1].append((ring_rank(peer, 4), ring_rank(xi, 4), {"dp": zi * 4 + peer}))
+            peer = lax.rem(zi + d, 4)
+            groups[2].append((peer, zi, {"dp": peer * 4 + xi}))
+    for peer in (pnext, pprev):
+        groups[3].append((peer, pipe, {"pipe": peer}))
 
     barrier = pltpu.get_barrier_semaphore()
-    greeted = [{"seq": lax.rem(me + d, n_seq)} for d in range(1, n_seq)]
-    greeted += [{"pipe": pnext}, {"pipe": pprev}]
-    if n_dp == 16:
-        greeted += [{"dp": peer} for peer in x_peers + z_peers]
-    for peer in greeted:
-        pl.semaphore_signal(barrier, inc=1, device_id=peer, device_id_type=MESH)
+    for peer in (nxt, prv):
+        pl.semaphore_signal(barrier, inc=1, device_id={"seq": peer}, device_id_type=MESH)
+    elders = 2
+    for group in groups:
+        for rank, own, peer in group:
+            elders = elders + jnp.where(rank < own, 1, 0)
+
+            @pl.when(rank > own)
+            def _():
+                pl.semaphore_signal(barrier, inc=1, device_id=peer, device_id_type=MESH)
+
+    def await_younger(i):
+        younger = sum(jnp.where(rank > own, 1, 0) for rank, own, _ in groups[i])
+
+        @pl.when(younger > 0)
+        def _():
+            pl.semaphore_wait(hello.at[i], younger)
 
     def columns(c):
         return pl.ds(pl.multiple_of(c * WIDE, WIDE), WIDE)
@@ -95,9 +120,15 @@
     def forward_halo(c):
         return halo_copy(fx_ref, c, c + CHUNKS)
 
-    pl.semaphore_wait(barrier, len(greeted))
-    for c in range(AHEAD - 1):
+    pl.semaphore_wait(barrier, elders)
+    for c in range(AHEAD):
         saved_halo(c).start()
+    for i, group in enumerate(groups):
+        for rank, own, peer in group:
+
+            @pl.when(rank < own)
+            def _():
+                pl.semaphore_signal(hello.at[i], inc=1, device_id=peer, device_id_type=MESH)
 
     def inverse_root(target):
         def add(c, total):
@@ -126,7 +157,8 @@
         device_id_type=MESH,
     )
     stat_copy.start()
-    saved_halo(AHEAD - 1).start()
+    for c in range(AHEAD, CHUNKS):
+        saved_halo(c).start()
 
     for copy in copies[2 * CHUNKS :]:
         copy.wait()
@@ -221,36 +253,27 @@
         part_send[c, 6:7, :] = biases[0]
         part_send[c, 7:8, :] = biases[1]
 
-        @pl.when(c != me)
+        @pl.when(c == 1)
+        def _():
+            await_younger(0)
+
+        @pl.when((c == 1) & (me != 0))
+        def _():
+            part_copy(0, me, 0).start()
+
+        @pl.when((c >= 1) & (c != me))
         def _():
             part_copy(c, me, c).start()
 
-        @pl.when(c < CHUNKS - AHEAD)
-        def _():
-            saved_halo(c + AHEAD).start()
-
-        @pl.when(c >= CHUNKS - AHEAD)
-        def _():
-            forward_halo(c + AHEAD - CHUNKS).start()
-
         return carry
 
     lax.fori_loop(0, CHUNKS, backward_chunk, 0)
-
-    def start_forward_halo(c, carry):
-        forward_halo(c).start()
-        return carry
-
-    lax.fori_loop(AHEAD, CHUNKS, start_forward_halo, 0)
 
     def fold(c, total):
         fold_copy(c).wait_recv()
         scaled_grad = (grads[c] + crecv[c].astype(f32)) * ng[:, columns(c)]
         grads[c] = scaled_grad
         return total + scaled_grad * (sx[c].astype(f32) * inv_s[...])
-
-    total = lax.fori_loop(0, CHUNKS, fold, jnp.zeros((BLOCK, WIDE), f32))
-    mean = jnp.broadcast_to(jnp.sum(total, axis=1, keepdims=True) / D, (BLOCK, WIDE))
 
     def bwd_copy(c):
         return pltpu.make_async_remote_copy(
@@ -268,8 +291,6 @@
         bsend[c] = (og[c].astype(f32) + root * (grads[c] - scaled * carry)).astype(bf16)
         bwd_copy(c).start()
         return carry
-
-    lax.fori_loop(0, CHUNKS, finish, mean)
 
     def fwd_copy(c):
         return pltpu.make_async_remote_copy(
@@ -318,7 +339,7 @@
             dst_ref=xs.at[xi],
             send_sem=xs_send.at[i],
             recv_sem=xs_recv.at[xi],
-            device_id={"dp": x_peers[i]},
+            device_id=groups[1][i][2],
             device_id_type=MESH,
         )
 
@@ -329,41 +350,63 @@
             dst_ref=xs.at[slot],
             send_sem=xs_send.at[i],
             recv_sem=xs_recv.at[slot],
-            device_id={"dp": x_peers[i]},
+            device_id=groups[1][i][2],
             device_id_type=MESH,
         )
 
     def z_copy(i):
         return pltpu.make_async_remote_copy(
-            src_ref=zs.at[i],
-            dst_ref=zr.at[i],
+            src_ref=zs.at[zi],
+            dst_ref=zs.at[zi],
             send_sem=z_send.at[i],
-            recv_sem=z_recv.at[i],
-            device_id={"dp": z_peers[i]},
-            device_id_type=MESH,
-        )
-
-    lax.fori_loop(0, 3, forward_chunk, 0)
+            recv_sem=z_recv.at[zi],
+            device_id=groups[2][i][2],
+            device_id_type=MESH,
+        )
+
+    def z_arrival(i):
+        slot = lax.rem(zi + i + 1, 4)
+        return pltpu.make_async_remote_copy(
+            src_ref=zs.at[slot],
+            dst_ref=zs.at[slot],
+            send_sem=z_send.at[i],
+            recv_sem=z_recv.at[slot],
+            device_id=groups[2][i][2],
+            device_id_type=MESH,
+        )
+
+    def z_start(to_elders):
+        for i, (rank, own, _) in enumerate(groups[2]):
+
+            @pl.when(rank < own if to_elders else rank > own)
+            def _():
+                z_copy(i).start()
+
+    total = lax.fori_loop(0, CHUNKS, fold, jnp.zeros((BLOCK, WIDE), f32))
+    mean = jnp.broadcast_to(jnp.sum(total, axis=1, keepdims=True) / D, (BLOCK, WIDE))
+
     total = seq_sum()
     if n_dp == 16:
         xs[xi] = total
+        await_younger(1)
         for i in range(3):
             x_copy(i).start()
-    lax.fori_loop(3, 5, forward_chunk, 0)
+    for c in range(CHUNKS):
+        forward_halo(c).start()
     if n_dp == 16:
         for i in range(3):
             x_arrival(i).wait_recv()
-        zs[0] = (xs[0] + xs[1]) + (xs[2] + xs[3])
-        z_copy(0).start()
-    lax.fori_loop(5, CHUNKS - 1, forward_chunk, 0)
+        zs[zi] = (xs[0] + xs[1]) + (xs[2] + xs[3])
+        z_start(True)
+    await_younger(3)
+    lax.fori_loop(0, CHUNKS, finish, mean)
+    lax.fori_loop(0, CHUNKS, forward_chunk, 0)
     if n_dp == 16:
-        z_copy(0).wait_recv()
-        zs[1] = zs[0] + zr[0]
-        z_copy(1).start()
-    lax.fori_loop(CHUNKS - 1, CHUNKS, forward_chunk, 0)
-    if n_dp == 16:
-        z_copy(1).wait_recv()
-        total = zs[1] + zr[1]
+        await_younger(2)
+        z_start(False)
+        for i in range(3):
+            z_arrival(i).wait_recv()
+        total = (zs[0] + zs[1]) + (zs[2] + zs[3])
 
     total = total * (1.0 / BATCH)
     gain, query_s, key_s, value_s = gains_of(me)
@@ -380,7 +423,6 @@
     if n_dp == 16:
         for i in range(3):
             x_copy(i).wait_send()
-        for i in range(2):
             z_copy(i).wait_send()
     for d in range(1, n_seq):
         peer = lax.rem(me + d, n_seq)
@@ -430,11 +472,12 @@
                 wide, wide, wide, wide, window, window, window,
                 pltpu.VMEM(tile, f32), pltpu.VMEM(tile, f32),
                 pltpu.VMEM((CHUNKS,) + tile, f32), pltpu.VMEM((CHUNKS,) + tile, f32),
-                pltpu.VMEM((4,) + tile, f32), pltpu.VMEM((2,) + tile, f32), pltpu.VMEM((2,) + tile, f32),
+                pltpu.VMEM((4,) + tile, f32), pltpu.VMEM((4,) + tile, f32),
                 sem((3 * CHUNKS + 6,)), sem((2 * CHUNKS,)), sem((2 * CHUNKS,)), sem((CHUNKS,)), sem((CHUNKS,)),
                 sem((2,)), sem((CHUNKS,)), sem((CHUNKS,)),
-                sem((3,)), sem((4,)), sem((2,)), sem((2,)),
+                sem((3,)), sem((4,)), sem((3,)), sem((4,)),
                 sem((CHUNKS,)), sem((CHUNKS,)), sem((CHUNKS,)), sem((CHUNKS,)),
+                pltpu.SemaphoreType.REGULAR((4,)),
             ],
             compiler_params=pltpu.CompilerParams(collective_id=0, has_side_effects=True),
             name="relay_tick",

time: 66 us -> 58.4 us (0.88)
  the two profiles are of different devices: /device:TPU:6 before, /device:TPU:1 now
where the time goes in v2:
time: 58.4 us; the launch traced here: 58.2 us
  Pallas kernels  53.6 us (92%)
  local copies, waits for them, and re-layouts  3.91 us (7%)
  between operations  0.65 us (1%)
    pallas_call x1, Pallas kernels, on_device(): pl.pallas_call(functools.partial(kernel, sizes), out_shape=(jax.ShapeDtyp...  53.6 us
    unnamed x10, local copies, waits for them, and re-layouts  3.91 us

profile of v2, /device:TPU:1, one launch (start us, length us, event | category | flops | bytes accessed | tf_op | source)
XLA Modules:
  0.0 58.2 jit_solution(2684542593425324298)
XLA Ops:
  0.6 53.6 %relay_tick.1 = (bf16[128,2048]{1,0:T(8,128)(2,1)}, bf16[128,2048]{1,0:T(8,128)(2,1)}, f32[4,256]{1,0:T(4,128)}, f32[1,2]{1,0:T(1,128)}) custom-call(bf16[128,2048]{1,0:T(8,128)(2,1)} %bitcast.8, bf16[128,2048]{1,0:T(8,128)(2,1)} %bitcast.9, bf16[128,2048]{1,0:T(8,128)(2,1)} %bitcast.10, s32[1,1024]{1,0:T(1,128)} %bitcast.13, s32[1,1024]{1,0:T(1,128)} %bitcast.14, ...), custom_call_target="tpu_custom_call" | custom-call | tf_op jit(solution)/shard_map/relay_tick/pallas_call | solution.py:455
  54.2 0.0 copy-start
  54.3 1.9 %copy.18 = bf16[1,1,128,2048]{3,2,1,0:T(8,128)(2,1)} copy(bf16[1,1,128,2048]{3,2,1,0:T(8,128)(2,1)} %bitcast.12) | data formatting | bytes 1048576
  56.2 0.0 copy-done
  56.2 0.0 copy-start.1
  56.2 0.8 %copy.19 = bf16[1,1,128,2048]{3,2,1,0:T(8,128)(2,1)} copy(bf16[1,1,128,2048]{3,2,1,0:T(8,128)(2,1)S(1)} %bitcast.11) | data formatting | bytes 1048576
  57.0 0.0 copy-done.1
  57.0 0.0 copy-start.2
  57.0 0.6 %copy.20 = f32[1,4,256]{2,1,0:T(4,128)} copy(f32[1,4,256]{2,1,0:T(4,128)S(1)} %bitcast.15) | data formatting | bytes 8192
  57.6 0.1 copy-done.2
  57.7 0.5 copy.21
Async XLA Ops:
  54.2 2.0 %copy-start = (bf16[128,2048]{1,0:T(8,128)(2,1)S(1)}, bf16[128,2048]{1,0:T(8,128)(2,1)}, u32[]{:S(2)}) copy-start(bf16[128,2048]{1,0:T(8,128)(2,1)} %get-tuple-element.9) | copy-start | bytes 1572868
  56.2 0.8 %copy-start.1 = (f32[4,256]{1,0:T(4,128)S(1)}, f32[4,256]{1,0:T(4,128)}, u32[]{:S(2)}) copy-start(f32[4,256]{1,0:T(4,128)} %get-tuple-element.10) | copy-start | bytes 12292
  57.0 0.7 %copy-start.2 = (f32[1,2]{1,0:T(1,128)S(1)}, f32[1,2]{1,0:T(1,128)}, u32[]{:S(2)}) copy-start(f32[1,2]{1,0:T(1,128)} %get-tuple-element.19) | copy-start | bytes 28

commit v3 on v2

--- a/solution.py
+++ b/solution.py
@@ -29,6 +29,12 @@
 
 def column_of(row):
     return jnp.transpose(jnp.broadcast_to(row, (BLOCK, BLOCK)))
+
+
+def turn(i, at):
+    if isinstance(i, int):
+        return lax.rem(at + (2 * (i % 2) - 1) * ((CHUNKS - i) // 2) + CHUNKS, CHUNKS)
+    return lax.rem(at + (2 * lax.rem(i, 2) - 1) * lax.div(CHUNKS - i, 2) + CHUNKS, CHUNKS)
 
 
 def twice(square):
@@ -121,8 +127,8 @@
         return halo_copy(fx_ref, c, c + CHUNKS)
 
     pl.semaphore_wait(barrier, elders)
-    for c in range(AHEAD):
-        saved_halo(c).start()
+    for i in range(AHEAD):
+        saved_halo(turn(i, nxt)).start()
     for i, group in enumerate(groups):
         for rank, own, peer in group:
 
@@ -157,8 +163,8 @@
         device_id_type=MESH,
     )
     stat_copy.start()
-    for c in range(AHEAD, CHUNKS):
-        saved_halo(c).start()
+    for i in range(AHEAD, CHUNKS):
+        saved_halo(turn(i, nxt)).start()
 
     for copy in copies[2 * CHUNKS :]:
         copy.wait()
@@ -207,7 +213,8 @@
             device_id_type=MESH,
         )
 
-    def backward_chunk(c, carry):
+    def backward_chunk(i, carry):
+        c = turn(i, me)
         saved_halo(c).wait_recv()
         gain, query_s, key_s, value_s = gains_of(c)
         scaled = sx[c].astype(f32) * inv_s[...]
@@ -247,27 +254,27 @@
             jnp.sum(key_a * scaled + key_b * scaled_p, axis=0, keepdims=True),
             jnp.sum(value_a * scaled + value_b * scaled_p, axis=0, keepdims=True),
         )
-        for i, row in enumerate(sums):
-            part_send[c, 2 * i : 2 * i + 1, :] = row[:, :HEAD_DIM]
-            part_send[c, 2 * i + 1 : 2 * i + 2, :] = row[:, HEAD_DIM:]
+        for j, row in enumerate(sums):
+            part_send[c, 2 * j : 2 * j + 1, :] = row[:, :HEAD_DIM]
+            part_send[c, 2 * j + 1 : 2 * j + 2, :] = row[:, HEAD_DIM:]
         part_send[c, 6:7, :] = biases[0]
         part_send[c, 7:8, :] = biases[1]
 
-        @pl.when(c == 1)
+        @pl.when(i == 1)
         def _():
             await_younger(0)
-
-        @pl.when((c == 1) & (me != 0))
-        def _():
-            part_copy(0, me, 0).start()
-
-        @pl.when((c >= 1) & (c != me))
+            first = turn(0, me)
+            part_copy(first, me, first).start()
+
+        @pl.when((i >= 1) & (i < CHUNKS - 1))
         def _():
             part_copy(c, me, c).start()
 
         return carry
 
     lax.fori_loop(0, CHUNKS, backward_chunk, 0)
+    for c in range(CHUNKS):
+        forward_halo(c).start()
 
     def fold(c, total):
         fold_copy(c).wait_recv()
@@ -382,17 +389,15 @@
             def _():
                 z_copy(i).start()
 
-    total = lax.fori_loop(0, CHUNKS, fold, jnp.zeros((BLOCK, WIDE), f32))
-    mean = jnp.broadcast_to(jnp.sum(total, axis=1, keepdims=True) / D, (BLOCK, WIDE))
-
     total = seq_sum()
     if n_dp == 16:
         xs[xi] = total
         await_younger(1)
         for i in range(3):
             x_copy(i).start()
-    for c in range(CHUNKS):
-        forward_halo(c).start()
+    mix = lax.fori_loop(0, CHUNKS, fold, jnp.zeros((BLOCK, WIDE), f32))
+    mean = jnp.broadcast_to(jnp.sum(mix, axis=1, keepdims=True) / D, (BLOCK, WIDE))
+
     if n_dp == 16:
         for i in range(3):
             x_arrival(i).wait_recv()
@@ -439,6 +444,15 @@
     lax.fori_loop(0, CHUNKS, drain, 0)
 
 
+def hand_out(*refs):
+    sources, targets, sems = refs[:4], refs[4:8], refs[8]
+    copies = [pltpu.make_async_copy(sources[i], targets[i], sems.at[i]) for i in range(4)]
+    for copy in copies:
+        copy.start()
+    for copy in copies:
+        copy.wait()
+
+
 def solution(mesh):
     sizes = tuple(mesh.shape[name] for name in ("dp", "pipe", "seq"))
     rows = (BLOCK, D)
@@ -452,16 +466,12 @@
         window = pltpu.VMEM((2 * BLOCK, BLOCK), f32)
         tile = (8, 128)
         sem = pltpu.SemaphoreType.DMA
-        fo, bo, sg, bg = pl.pallas_call(
+        results = ((rows, bf16), (rows, bf16), ((4, WIDE), f32), ((1, 2), f32))
+        held = pl.pallas_call(
             functools.partial(kernel, sizes),
-            out_shape=(
-                jax.ShapeDtypeStruct(rows, bf16),
-                jax.ShapeDtypeStruct(rows, bf16),
-                jax.ShapeDtypeStruct((4, WIDE), f32),
-                jax.ShapeDtypeStruct((1, 2), f32),
-            ),
+            out_shape=tuple(pltpu.VMEM(*result) for result in results),
             in_specs=[hbm] * 9 + [smem],
-            out_specs=(hbm, hbm, vmem, vmem),
+            out_specs=(vmem, vmem, vmem, vmem),
             scratch_shapes=[
                 chunked, chunked, chunked,
                 pltpu.VMEM((2 * CHUNKS, BLOCK, WIDE), bf16),
@@ -486,6 +496,14 @@
             fwd_sky.reshape(1, -1), bwd_sky.reshape(1, -1),
             norm_gain, query_scale, key_scale, value_scale, sky_bias,
         )
+        fo, bo, sg, bg = pl.pallas_call(
+            hand_out,
+            out_shape=tuple(jax.ShapeDtypeStruct(*result) for result in results),
+            in_specs=[pl.BlockSpec(memory_space=pl.ANY)] * 4,
+            out_specs=(hbm,) * 4,
+            scratch_shapes=[sem((4,))],
+            name="hand_out",
+        )(*(pltpu.with_memory_space_constraint(x, pltpu.MemorySpace.VMEM) for x in held))
         return fo[None, None], bo[None, None], sg[None], bg
 
     placed = (

time: 58.4 us -> 51.6 us (0.88)
  local copies, waits for them, and re-layouts: 3.91 us -> 0 us
  Pallas kernels: 53.6 us -> 50.8 us
    unnamed x10 -> x0, local copies, waits for them, and re-layouts: 3.91 us -> none
    pallas_call x1 -> x2, Pallas kernels: 53.6 us -> 50.8 us  [the longest x1 49.8 us: on_device(): pl.pallas_call(functools.partial(kernel, sizes), out_shape=tuple((pltpu.V...]
where the time goes in v3:
time: 51.6 us; the launch traced here: 51.4 us
  Pallas kernels  50.8 us (98%)
  between operations  0.64 us (1%)
    pallas_call x1, Pallas kernels, on_device(): pl.pallas_call(functools.partial(kernel, sizes), out_shape=tuple((pltpu.V...  49.8 us

profile of v3, /device:TPU:1, one launch (start us, length us, event | category | flops | bytes accessed | tf_op | source)
XLA Modules:
  0.0 51.4 jit_solution(12897410676342055828)
XLA Ops:
  0.6 49.8 %relay_tick.1 = (bf16[128,2048]{1,0:T(8,128)(2,1)S(1)}, bf16[128,2048]{1,0:T(8,128)(2,1)S(1)}, f32[4,256]{1,0:T(4,128)S(1)}, f32[1,2]{1,0:T(1,128)S(1)}) custom-call(bf16[128,2048]{1,0:T(8,128)(2,1)} %bitcast.8, bf16[128,2048]{1,0:T(8,128)(2,1)} %bitcast.9, bf16[128,2048]{1,0:T(8,128)(2,1)} %bitcast.10, s32[1,1024]{1,0:T(1,128)} %bitcast.11, ...), custom_call_target="tpu_custom_call" | custom-call | tf_op jit(solution)/shard_map/relay_tick/pallas_call | solution.py:470
  50.4 1.0 %hand_out.1 = (bf16[128,2048]{1,0:T(8,128)(2,1)}, bf16[128,2048]{1,0:T(8,128)(2,1)}, f32[4,256]{1,0:T(4,128)}, f32[1,2]{1,0:T(1,128)}) custom-call(bf16[128,2048]{1,0:T(8,128)(2,1)S(1)} %get-tuple-element.12.refs_0_, bf16[128,2048]{1,0:T(8,128)(2,1)S(1)} %get-tuple-element.13.refs_1_, f32[4,256]{1,0:T(4,128)S(1)} %get-tuple-element.14.refs_2_, ...), custom_call_target="tpu_custom_call" | custom-call | tf_op jit(solution)/shard_map/hand_out/pallas_call | solution.py:499

commit v4 on v3

--- a/solution.py
+++ b/solution.py
@@ -270,11 +270,14 @@
         def _():
             part_copy(c, me, c).start()
 
+        @pl.when(i == CHUNKS - 2)
+        def _():
+            for later in range(CHUNKS):
+                forward_halo(later).start()
+
         return carry
 
     lax.fori_loop(0, CHUNKS, backward_chunk, 0)
-    for c in range(CHUNKS):
-        forward_halo(c).start()
 
     def fold(c, total):
         fold_copy(c).wait_recv()

time: 51.6 us -> 51.4 us (level)
  no operation moved by 1% of the time
where the time goes in v4:
time: 51.4 us; the launch traced here: 51.1 us
  Pallas kernels  50.5 us (98%)
  between operations  0.64 us (1%)
    pallas_call x1, Pallas kernels, on_device(): pl.pallas_call(functools.partial(kernel, sizes), out_shape=tuple((pltpu.V...  49.5 us

profile of v4, /device:TPU:1, one launch (start us, length us, event | category | flops | bytes accessed | tf_op | source)
XLA Modules:
  0.0 51.1 jit_solution(2492114187753418794)
XLA Ops:
  0.6 49.5 %relay_tick.1 = (bf16[128,2048]{1,0:T(8,128)(2,1)S(1)}, bf16[128,2048]{1,0:T(8,128)(2,1)S(1)}, f32[4,256]{1,0:T(4,128)S(1)}, f32[1,2]{1,0:T(1,128)S(1)}) custom-call(bf16[128,2048]{1,0:T(8,128)(2,1)} %bitcast.8, bf16[128,2048]{1,0:T(8,128)(2,1)} %bitcast.9, bf16[128,2048]{1,0:T(8,128)(2,1)} %bitcast.10, s32[1,1024]{1,0:T(1,128)} %bitcast.11, ...), custom_call_target="tpu_custom_call" | custom-call | tf_op jit(solution)/shard_map/relay_tick/pallas_call | solution.py:473
  50.1 1.0 %hand_out.1 = (bf16[128,2048]{1,0:T(8,128)(2,1)}, bf16[128,2048]{1,0:T(8,128)(2,1)}, f32[4,256]{1,0:T(4,128)}, f32[1,2]{1,0:T(1,128)}) custom-call(bf16[128,2048]{1,0:T(8,128)(2,1)S(1)} %get-tuple-element.12.refs_0_, bf16[128,2048]{1,0:T(8,128)(2,1)S(1)} %get-tuple-element.13.refs_1_, f32[4,256]{1,0:T(4,128)S(1)} %get-tuple-element.14.refs_2_, ...), custom_call_target="tpu_custom_call" | custom-call | tf_op jit(solution)/shard_map/hand_out/pallas_call | solution.py:502
